TPU v7x, 256 devices: a whole 4x4x8 slice. The times are simulated.
256 devices in a mesh: rep: 2 (over core), req: 32 (over y, z), tp: 4 (over x).
Axes of the slice: x: 4, y: 4, z: 8, core: 2. Of those that a mesh axis runs over, the one named last changes fastest.
Arguments:
- hidden: bfloat16 [1024, 1536], P(('rep', 'req'), 'tp'), may hold values from -6 to 6
- lengths: int32 [2, 512], P(None, 'req'), may hold values from 16 to 1024, as said below
- migrate: int32 [32], P('req'), may hold values from 0 to 15
- kv_cache: bfloat16 [1024, 1024, 8, 128], P(('rep', 'req'), None, 'tp'), may hold values from -250 to 250
- attn_gain: float32 [1536], replicated, may hold values from 0.1 to 1.9
- moe_gain: float32 [1536], replicated, may hold values from 0.1 to 1.9
- w_query: bfloat16 [1536, 1536], P(None, 'tp'), may hold values from -0.15625 to 0.15625
- key_value_weight: bfloat16 [1536, 1024], P(None, 'tp'), may hold values from -0.15625 to 0.15625
- output_weight: bfloat16 [1536, 1536], P('tp'), may hold values from -0.25 to 0.25
- w_gateup: bfloat16 [64, 1536, 2, 512], P(('rep', 'req'), None, None, 'tp'), may hold values from -0.15625 to 0.15625
- w_down: bfloat16 [64, 512, 1536], P(('rep', 'req'), 'tp'), may hold values from -0.25 to 0.25
- expert_ids: int32 [1024, 8], P(('rep', 'req')), may hold values from 0 to 63, all different within a row; in each aligned block of 16 rows (0 to 15, 16 to 31, ...) at most 6 rows name the same one
- expert_gates: float32 [1024, 8], P(('rep', 'req')), may hold values from 0.1 to 0.4
Outputs:
- layer_out: bfloat16 [1024, 1536], P(('rep', 'req'), 'tp')
Inputs may be any that keep to these rules, and one draw needn't show every extreme that they name: A request attends to its first lengths positions and to its own new key. `expert_ids`: each row names 8 distinct experts; among the rows of one device (an aligned block of 16 rows) no expert is named more than 6 times, and in some blocks one expert is named exactly 6 times.
All inputs are finite; a program needn't handle non-finite values.
Results may differ from a plain program's by a relative error of at most 0.015.
Values may be sent and summed in bfloat16 or wider, within the bound.
A program may use at most 64 MiB of HBM per device.

v0:
```python
import jax
import jax.numpy as jnp
from jax import lax
from jax.sharding import PartitionSpec as P

HEAD_SIZE = 64
epsilon = 1e-06
rope_base = 10000.0
masked_score = -1e30


def swapped(value, axis, apart):
    return lax.ppermute(value, axis, [(i, i ^ 1 << apart) for i in range(lax.axis_size(axis))])


def rms_norm(values, gain):
    mean_square = jnp.mean(values * values, axis=-1, keepdims=True)
    return values * lax.rsqrt(mean_square + epsilon) * gain


def apply_rotation(values, position):
    half_width = values.shape[-1] // 2
    inv_freq = rope_base ** (-jnp.arange(half_width, dtype=jnp.float32) * 2.0 / values.shape[-1])
    angles = position.astype(jnp.float32)[:, None, None] * inv_freq
    cosine = jnp.cos(angles)
    sine_part = jnp.sin(angles)
    first_half = values[..., :half_width]
    second_half = values[..., half_width:]
    return jnp.concatenate(
        [
            first_half * cosine - second_half * sine_part,
            second_half * cosine + first_half * sine_part,
        ],
        axis=-1,
    )


def attention(
    token_part, kv_rows, request_extent, attn_gain, w_query, key_value_weight, output_weight
):
    tokens = lax.all_gather(token_part, "tp", axis=1, tiled=True)
    row_count = tokens.shape[0]
    head_dim = HEAD_SIZE
    local_kv = kv_rows.shape[2]
    local_query = w_query.shape[1] // head_dim
    group_size = local_query // local_kv
    normalized_input = rms_norm(tokens.astype(jnp.float32), attn_gain).astype(jnp.bfloat16)
    query_vectors = jnp.dot(normalized_input, w_query, preferred_element_type=jnp.float32).reshape(
        row_count, local_query, head_dim
    )
    key_value_rows = jnp.dot(
        normalized_input, key_value_weight, preferred_element_type=jnp.float32
    ).reshape(row_count, local_kv, 2 * head_dim)
    query_vectors = (
        apply_rotation(query_vectors, request_extent)
        .astype(jnp.bfloat16)
        .reshape(row_count, local_kv, group_size, head_dim)
    )
    key_new = apply_rotation(key_value_rows[..., :head_dim], request_extent).astype(jnp.bfloat16)
    value_new = key_value_rows[..., head_dim:].astype(jnp.bfloat16)
    score_scale = head_dim ** (-0.5)
    cache_keys = kv_rows[..., :head_dim]
    cache_values = kv_rows[..., head_dim:]
    scores = (
        jnp.einsum("rhgd,rthd->rhgt", query_vectors, cache_keys, preferred_element_type=jnp.float32)
        * score_scale
    )
    own_score = (
        jnp.einsum("rhgd,rhd->rhg", query_vectors, key_new, preferred_element_type=jnp.float32)
        * score_scale
    )
    positions = jnp.arange(kv_rows.shape[1], dtype=jnp.int32)
    visible = positions[None, None, None, :] < request_extent[:, None, None, None]
    scores = jnp.where(visible, scores, masked_score)
    row_peak = jnp.maximum(jnp.max(scores, axis=-1), own_score)
    cache_prob = jnp.exp(scores - row_peak[..., None])
    own_prob = jnp.exp(own_score - row_peak)
    denominator = jnp.sum(cache_prob, axis=-1) + own_prob
    cache_weight = (cache_prob / denominator[..., None]).astype(jnp.bfloat16)
    own_weight = (own_prob / denominator).astype(jnp.bfloat16)
    mixture = jnp.einsum(
        "rhgt,rthd->rhgd", cache_weight, cache_values, preferred_element_type=jnp.float32
    )
    mixture = (
        mixture
        + own_weight.astype(jnp.float32)[..., None] * value_new.astype(jnp.float32)[:, :, None, :]
    )
    context = mixture.reshape(row_count, local_query * head_dim).astype(jnp.bfloat16)
    partial_out = jnp.dot(context, output_weight, preferred_element_type=jnp.float32)
    return tokens.astype(jnp.float32) + lax.psum(partial_out.astype(jnp.bfloat16), "tp").astype(
        jnp.float32
    )


def shards(
    hidden,
    lengths,
    migrate,
    kv_cache,
    attn_gain,
    moe_gain,
    w_query,
    key_value_weight,
    output_weight,
    w_gateup,
    w_down,
    expert_ids,
    expert_gates,
):
    row_count = hidden.shape[0]
    replica = lax.axis_index("rep")
    slot_index = jnp.arange(row_count, dtype=jnp.int32)
    chosen_slot = migrate[0]
    is_moved = slot_index == chosen_slot
    own_span = lax.dynamic_index_in_dim(lengths, replica, 0, keepdims=False)
    other_span = lax.dynamic_index_in_dim(lengths, 1 - replica, 0, keepdims=False)
    picked_cache = lax.dynamic_slice_in_dim(kv_cache, chosen_slot, 1, 0)
    picked_row = lax.dynamic_slice_in_dim(hidden, chosen_slot, 1, 0)
    cache_width = picked_cache.size
    packed = jnp.concatenate([picked_cache.reshape(1, cache_width), picked_row], axis=1)
    arrived = swapped(packed, "rep", 0)
    moved_cache = arrived[:, :cache_width].reshape(picked_cache.shape)
    moved_row = arrived[:, cache_width:]
    served_cache = lax.dynamic_update_slice_in_dim(kv_cache, moved_cache, chosen_slot, 0)
    served_rows = lax.dynamic_update_slice_in_dim(hidden, moved_row, chosen_slot, 0)
    request_extent = jnp.where(is_moved, other_span, own_span)
    residual = attention(
        served_rows,
        served_cache,
        request_extent,
        attn_gain,
        w_query,
        key_value_weight,
        output_weight,
    )
    full_width = moe_gain.shape[0]
    quarter = full_width // lax.axis_size("tp")
    expert_in = rms_norm(residual, moe_gain).astype(jnp.bfloat16)
    own_residual = lax.dynamic_slice_in_dim(residual, lax.axis_index("tp") * quarter, quarter, 1)
    expert_count = lax.axis_size("rep") * lax.axis_size("req")
    top_count = expert_ids.shape[1]
    capacity = min(row_count, max(3, 3 * row_count * top_count // expert_count))
    flat_ids = expert_ids.reshape(-1)
    matches = (flat_ids[:, None] == jnp.arange(expert_count, dtype=jnp.int32)[None, :]).astype(
        jnp.int32
    )
    slot_rank = jnp.sum((jnp.cumsum(matches, axis=0) - matches) * matches, axis=1)
    slot_target = flat_ids * capacity + slot_rank
    slot_table = (
        slot_target[:, None] == jnp.arange(expert_count * capacity, dtype=jnp.int32)[None, :]
    ).astype(jnp.float32)
    route_table = slot_table.reshape(row_count, top_count, -1).sum(axis=1)
    gate_table = (
        (slot_table * expert_gates.reshape(-1, 1)).reshape(row_count, top_count, -1).sum(axis=1)
    )
    outbound = jnp.einsum(
        "rs,rd->sd", route_table.astype(jnp.bfloat16), expert_in, preferred_element_type=jnp.float32
    ).astype(jnp.bfloat16)
    outbound = outbound.reshape(expert_count, capacity, -1)
    gate_up = w_gateup[0].reshape(w_gateup.shape[1], -1)
    down_rows = w_down[0]
    arrived_rows = lax.all_to_all(outbound, ("rep", "req"), split_axis=0, concat_axis=0, tiled=True)
    model_width = arrived_rows.shape[2]
    flattened = arrived_rows.reshape(-1, model_width)
    projected = jnp.dot(flattened, gate_up, preferred_element_type=jnp.float32)
    split_at = projected.shape[1] // 2
    activation = (jax.nn.silu(projected[:, :split_at]) * projected[:, split_at:]).astype(
        jnp.bfloat16
    )
    expert_part = jnp.dot(activation, down_rows, preferred_element_type=jnp.float32)
    expert_part = expert_part.reshape(arrived_rows.shape[0], arrived_rows.shape[1], model_width)
    returned = lax.all_to_all(
        expert_part.astype(jnp.bfloat16), ("rep", "req"), split_axis=0, concat_axis=0, tiled=True
    ).astype(expert_part.dtype)
    returned_rows = returned.reshape(expert_count * capacity, -1)
    combined = jnp.dot(
        gate_table,
        returned_rows,
        precision=lax.Precision.HIGHEST,
        preferred_element_type=jnp.float32,
    )
    expert_mix = lax.psum_scatter(
        combined.astype(jnp.bfloat16), "tp", scatter_dimension=1, tiled=True
    ).astype(jnp.float32)
    return (own_residual + expert_mix).astype(jnp.bfloat16)


def solution(mesh):
    placed = (
        P(("rep", "req"), "tp"),
        P(None, "req"),
        P("req"),
        P(("rep", "req"), None, "tp", None),
        P(),
        P(),
        P(None, "tp"),
        P(None, "tp"),
        P("tp", None),
        P(("rep", "req"), None, None, "tp"),
        P(("rep", "req"), "tp", None),
        P(("rep", "req"), None),
        P(("rep", "req"), None),
    )
    return jax.shard_map(
        shards, mesh=mesh, in_specs=placed, out_specs=P(("rep", "req"), "tp"), check_vma=False
    )
```

profile of v0, /device:TPU:8, one launch (start us, length us, event | category | flops | bytes accessed | tf_op | source)
XLA Modules:
  0.0 226.3 jit_solution(14845780851035790938)
XLA Ops:
  6.5 0.8 copy.69
  8.0 1.4 constant_dynamic-slice_fusion.3
  9.6 4.4 %pad_maximum_fusion = bf16[1,262528]{1,0:T(2,128)(2,1)S(1)} fusion(bf16[1,384]{1,0:T(2,128)(2,1)S(1)} %constant_dynamic-slice_fusion.2, bf16[1,262144]{1,0:T(2,128)(2,1)S(1)} %reshape.200), kind=kLoop, calls=%fused_computation.12 | loop fusion | flops 1050112 | bytes 1050112 | tf_op jit(solution)/shard_map/concatenate | solution.py:120
  14.2 21.2 %copy.45 = bf16[16,1024,2,128]{1,3,2,0:T(8,128)(2,1)} copy(bf16[16,1024,2,128]{3,2,1,0:T(2,128)(2,1)} %param.16) | data formatting | bytes 16777216 | tf_op args[3]
  36.6 1.0 copy-done.2
  37.7 12.2 %all_gather.3 = bf16[16,1536]{1,0:T(8,128)(2,1)S(1)} all-gather(bf16[16,384]{1,0:T(8,128)(2,1)S(1)} %dynamic_update_slice.6), channel_id=1, replica_groups=mesh['rep'=2,'req'=32,'tp'=4] {'tp'}, dimensions={1}, use_global_device_ids=true | all-gather | bytes 61440 | tf_op jit(solution)/shard_map/all_gather | solution.py:41
  49.9 9.9 %slice_reduce_fusion = bf16[262144]{0:T(1024)(128)(2,1)S(1)} fusion(bf16[1,262528]{1,0:T(2,128)(2,1)} %copy-done.2), kind=kLoop, calls=%fused_computation.13 | loop fusion | bytes 1048576 | tf_op jit(solution)/shard_map/slice | solution.py:122
  60.8 1.4 fusion.34
  62.5 0.9 constant_dynamic-update-slice_fusion
  63.7 3.0 %fusion.44 = (f32[16,2,3]{2,1,0:T(2,128)S(1)}, f32[16,2,3,1024]{3,2,1,0:T(4,128)S(1)}) fusion(bf16[16,1024,2,128]{1,3,2,0:T(8,128)(2,1)} %constant_dynamic-update-slice_fusion, bf16[16,2,3,32]{3,2,1,0:T(4,128)(2,1)S(1)} %copy.44, bf16[16,2,3,32]{3,2,1,0:T(4,128)(2,1)S(1)} %copy.43, pred[16,1024]{1,0:T(8,128)(4,1)S(1)} %iota_compare_fusion.2), kind=kOutput, calls=%fused_computation.77 | convolution fusion | flops 12902304 | bytes 4616576 | tf_op jit(solution)/shard_map/rhgd,rthd->rhgt/dot_general | solution.py:65
  67.2 3.5 %fusion.13 = bf16[16,2,3,64]{3,2,1,0:T(4,128)(2,1)S(1)} fusion(bf16[16,1024,2,128]{1,3,2,0:T(8,128)(2,1)} %constant_dynamic-update-slice_fusion, f32[16,2,3,1024]{3,2,1,0:T(4,128)S(1)} %get-tuple-element.20, f32[16,2,3]{2,1,0:T(2,128)S(1)} %get-tuple-element.14, f32[16,2,3]{2,1,0:T(2,128)S(1)} %multiply_maximum_fusion, f32[16,2,64]{2,1,0:T(2,128)S(1)} %fusion.38, ...), kind=kOutput, calls=%fused_computation.11 | convolution fusion | flops 12896256 | bytes 4609152 | tf_op jit(solution)/shard_map/rhgt,rthd->rhgd/dot_general | solution.py:81
  71.0 17.0 %psum.7 = bf16[16,1536]{1,0:T(8,128)(2,1)S(1)} all-reduce(bf16[16,1536]{1,0:T(8,128)(2,1)S(1)} %convolution_convert_fusion.3), channel_id=1, replica_groups=mesh['rep'=2,'req'=32,'tp'=4] {'tp'}, use_global_device_ids=true, to_apply=%region_3.4 | all-reduce | flops 24576 | bytes 98304 | tf_op jit(solution)/shard_map/psum | solution.py:90
  88.2 1.5 convolution_convert_fusion
  89.7 2.2 reshape.204
  91.9 51.9 %all_to_all.10 = bf16[64,6,1536]{2,1,0:T(8,128)(2,1)} all-to-all(bf16[64,6,1536]{2,1,0:T(8,128)(2,1)S(1)} %reshape.204), channel_id=1, replica_groups=mesh['rep'=2,'req'=32,'tp'=4] {'rep','req'}, dimensions={0} | all-to-all | bytes 2359296 | tf_op jit(solution)/shard_map/all_to_all | solution.py:162
  143.8 2.3 %reshape.205 = bf16[384,1536]{1,0:T(8,128)(2,1)S(1)} reshape(bf16[64,6,1536]{2,1,0:T(8,128)(2,1)} %all_to_all.10) | data formatting | bytes 2359296 | tf_op jit(solution)/shard_map/reshape | solution.py:164
  146.1 1.7 fusion.16
  148.4 0.7 copy.51
  149.0 45.9 %all_to_all.11 = bf16[64,6,1536]{2,1,0:T(8,128)(2,1)S(1)} all-to-all(bf16[64,6,1536]{2,1,0:T(8,128)(2,1)S(1)} %copy.51), channel_id=1, replica_groups=mesh['rep'=2,'req'=32,'tp'=4] {'rep','req'}, dimensions={0} | all-to-all | bytes 2359296 | tf_op jit(solution)/shard_map/all_to_all | solution.py:172
  195.0 1.2 reshape.206
  196.2 1.8 convolution_convert_fusion.2
  198.0 0.9 copy.54
  199.0 18.9 %reduce-scatter.4.cloned.1.call-done = bf16[384,16]{1,0:T(8,128)(2,1)} async-done(((bf16[1536,16]{1,0:T(8,128)(2,1)}), bf16[384,16]{1,0:T(8,128)(2,1)}) %reduce-scatter.4.cloned.1.call-update) | async-done | bytes 12304
  217.9 1.0 copy.55
  (64 shorter events, 5.2 us)
Async XLA Ops:
  6.5 64.2 %copy-start = (bf16[384,1536]{1,0:T(8,128)(2,1)S(1)}, bf16[384,1536]{1,0:T(8,128)(2,1)}, u32[]{:S(2)}) copy-start(bf16[384,1536]{1,0:T(8,128)(2,1)} %param.21) | copy-start | bytes 3538948
  6.5 211.4 %reduce-scatter.4.cloned.1.call-start = ((), (), s32[]{:S(2)}) async-start(), calls=%async_computation.3 | async-start | bytes 491520
  14.0 21.3 %copy-start.6 = (s32[16,8]{0,1:T(8,128)S(1)}, s32[16,8]{0,1:T(8,128)}, u32[]{:S(2)}) copy-start(s32[16,8]{0,1:T(8,128)} %param.24) | copy-start | bytes 1540
  14.1 22.0 %copy-start.7 = (f32[16,8]{0,1:T(8,128)S(1)}, f32[16,8]{0,1:T(8,128)}, u32[]{:S(2)}) copy-start(f32[16,8]{0,1:T(8,128)} %param.25) | copy-start | bytes 1540
  14.1 22.3 %copy-start.8 = (s32[2,16]{1,0:T(2,128)S(1)}, s32[2,16]{1,0:T(2,128)}, u32[]{:S(2)}) copy-start(s32[2,16]{1,0:T(2,128)} %param.14) | copy-start | bytes 388
  14.1 22.5 %collective-permute-start = (bf16[1,262528]{1,0:T(2,128)(2,1)S(1)}, bf16[1,262528]{1,0:T(2,128)(2,1)S(1)}, u32[]{:S(2)}, u32[]{:S(2)}) collective-permute-start(bf16[1,262528]{1,0:T(2,128)(2,1)S(1)} %pad_maximum_fusion), channel_id=1, source_target_pairs={{0,128},{128,0},{1,129},{129,1},{2,130},{130,2},{3,131},{131,3},{4... | collective-permute-start | bytes 1575176 | tf_op jit(solution)/shard_map/ppermute | solution.py:13
  36.6 1.1 copy-start.2
  49.9 10.4 %copy-start.1 = (bf16[1536,384]{1,0:T(8,128)(2,1)S(1)}, bf16[1536,384]{1,0:T(8,128)(2,1)}, u32[]{:S(2)}) copy-start(bf16[1536,384]{1,0:T(8,128)(2,1)} %param.19) | copy-start | bytes 3538948
  49.9 10.4 %copy-start.4 = (f32[1536]{0:T(1024)S(1)}, f32[1536]{0:T(1024)}, u32[]{:S(2)}) copy-start(f32[1536]{0:T(1024)} %param.17) | copy-start | bytes 18436
  70.6 17.6 %copy-start.5 = (f32[1536]{0:T(1024)S(1)}, f32[1536]{0:T(1024)}, u32[]{:S(2)}) copy-start(f32[1536]{0:T(1024)} %param.18) | copy-start | bytes 18436
  146.1 1.8 copy-start.3
Sparse Core Ops, SparseCore 0:
  199.1 18.7 reduce-scatter.3
where the time goes:
time: 227 us; the launch traced here: 226 us
  blocking collectives  127 us (56%)
  local copies, waits for them, and re-layouts  44.7 us (20%)
  waiting for transfers between devices  18.9 us (8%)
  between operations  14.4 us (6%)
  matrix products  14.1 us (6%)
  other arithmetic  6.97 us (3%)
    all_to_all x1, blocking collectives, shards(): lax.all_to_all(outbound, ('rep', 'req'), split_axis=0, concat_axis=0, til...  51.9 us
    all_to_all x1, blocking collectives, shards(): lax.all_to_all(expert_part.astype(jnp.bfloat16), ('rep', 'req'), split_ax...  45.9 us
    unnamed x24, local copies, waits for them, and re-layouts  25.1 us
    unnamed x2, waiting for transfers between devices  18.9 us
    psum x1, blocking collectives, attention(): lax.psum(partial_out.astype(jnp.bfloat16), 'tp').astype(jnp.float32)  17 us
    all_gather x1, blocking collectives, attention(): tokens = lax.all_gather(token_part, 'tp', axis=1, tiled=True)  12.2 us
    slice x1, local copies, waits for them, and re-layouts, shards(): moved_cache = arrived[:, :cache_width].reshape(picked_cache.shape)  9.86 us
  transfers between devices with their start and end apart: 2, of which 1 were waited for; matrix products, arithmetic and copies ran while one was open for 10% of the time, Pallas kernels for 0%

commit v1 on v0

--- a/solution.py
+++ b/solution.py
@@ -38,7 +38,9 @@
 def attention(
     token_part, kv_rows, request_extent, attn_gain, w_query, key_value_weight, output_weight
 ):
-    tokens = lax.all_gather(token_part, "tp", axis=1, tiled=True)
+    tokens = jnp.concatenate(
+        lax.all_to_all(jnp.stack([token_part] * lax.axis_size("tp")), "tp", 0, 0), axis=1
+    )
     row_count = tokens.shape[0]
     head_dim = HEAD_SIZE
     local_kv = kv_rows.shape[2]

time: 227 us -> 224 us (0.987)
  blocking collectives: 127 us -> 116 us
  local copies, waits for them, and re-layouts: 44.7 us -> 50.2 us
  starting transfers between devices: 0.09 us -> 4.3 us
  matrix products: 14.1 us -> 11.7 us
    all_gather x1 -> x0, blocking collectives: 12.2 us -> none  [attention(): tokens = lax.all_gather(token_part, 'tp', axis=1, tiled=True)]
    all_to_all x0 -> x1, starting transfers between devices: none -> 4.29 us  [attention(): lax.all_to_all(jnp.stack([token_part] * lax.axis_size('tp')), 'tp', 0, 0)]
    unnamed x24 -> x25, local copies, waits for them, and re-layouts: 25.1 us -> 25.7 us
  transfers between devices with their start and end apart: 2 -> 3, of which waited for: 1 -> 1; matrix products, arithmetic and copies ran while one was open for 10% -> 17% of each run, Pallas kernels for 0% -> 0%
where the time goes in v1:
time: 224 us; the launch traced here: 223 us
  blocking collectives  116 us (52%)
  local copies, waits for them, and re-layouts  50.2 us (22%)
  waiting for transfers between devices  19 us (8%)
  between operations  14.4 us (6%)
  matrix products  11.7 us (5%)
  other arithmetic  7.8 us (3%)
  starting transfers between devices  4.3 us (2%)
    all_to_all x1, blocking collectives, shards(): lax.all_to_all(outbound, ('rep', 'req'), split_axis=0, concat_axis=0, til...  51.9 us
    all_to_all x1, blocking collectives, shards(): lax.all_to_all(expert_part.astype(jnp.bfloat16), ('rep', 'req'), split_ax...  45.9 us
    unnamed x25, local copies, waits for them, and re-layouts  25.7 us
    unnamed x2, waiting for transfers between devices  19 us
    psum x1, blocking collectives, attention(): lax.psum(partial_out.astype(jnp.bfloat16), 'tp').astype(jnp.float32)  17.9 us
    slice x1, local copies, waits for them, and re-layouts, shards(): moved_cache = arrived[:, :cache_width].reshape(picked_cache.shape)  10.6 us
    concatenate x1, other arithmetic, shards(): jnp.concatenate([picked_cache.reshape(1, cache_width), picked_row], axis=1)  5.14 us
  transfers between devices with their start and end apart: 3, of which 1 were waited for; matrix products, arithmetic and copies ran while one was open for 17% of the time, Pallas kernels for 0%

profile of v1, /device:TPU:8, one launch (start us, length us, event | category | flops | bytes accessed | tf_op | source)
XLA Modules:
  0.0 223.1 jit_solution(6973093702660996492)
XLA Ops:
  6.5 0.8 copy.96
  8.0 1.4 constant_dynamic-slice_fusion.3
  9.6 5.1 %pad_maximum_fusion = bf16[1,262528]{1,0:T(2,128)(2,1)} fusion(bf16[1,384]{1,0:T(2,128)(2,1)S(1)} %constant_dynamic-slice_fusion.2, bf16[1,262144]{1,0:T(2,128)(2,1)S(1)} %reshape.230), kind=kLoop, calls=%fused_computation.12 | loop fusion | flops 1050112 | bytes 1050112 | tf_op jit(solution)/shard_map/concatenate | solution.py:122
  14.8 21.2 %copy.68 = bf16[16,1024,2,128]{1,3,2,0:T(8,128)(2,1)} copy(bf16[16,1024,2,128]{3,2,1,0:T(2,128)(2,1)} %param.16) | data formatting | bytes 16777216 | tf_op args[3]
  36.3 1.6 copy.65
  39.2 0.7 slice.48
  40.5 4.3 %all-to-all-start = ((bf16[4,16,384]{2,1,0:T(8,128)(2,1)}), bf16[4,16,384]{2,1,0:T(8,128)(2,1)S(1)}, u32[]{:S(2)}, u32[]{:S(2)}) async-start(bf16[4,16,384]{2,1,0:T(8,128)(2,1)} %stack.2), calls=%async_computation | async-start | bytes 98304 | tf_op jit(solution)/shard_map/all_to_all | solution.py:42
  44.8 10.6 %slice_reduce_fusion = bf16[262144]{0:T(1024)(128)(2,1)} fusion(bf16[1,262528]{1,0:T(2,128)(2,1)} %collective-permute-done), kind=kLoop, calls=%fused_computation.13 | loop fusion | bytes 1048576 | tf_op jit(solution)/shard_map/slice | solution.py:124
  55.4 2.0 copy.69
  57.4 1.9 constant_dynamic-update-slice_fusion
  61.1 3.7 %fusion.41 = (f32[16,2,3]{2,1,0:T(2,128)S(1)}, f32[16,2,3,1024]{3,2,1,0:T(4,128)S(1)}) fusion(bf16[16,1024,2,128]{1,3,2,0:T(8,128)(2,1)} %constant_dynamic-update-slice_fusion, bf16[16,2,3,32]{3,2,1,0:T(4,128)(2,1)S(1)} %copy.67, bf16[16,2,3,32]{3,2,1,0:T(4,128)(2,1)S(1)} %copy.66, pred[16,1024]{1,0:T(8,128)(4,1)S(1)} %iota_compare_fusion.2), kind=kOutput, calls=%fused_computation.77 | convolution fusion | flops 12902304 | bytes 4616576 | tf_op jit(solution)/shard_map/rhgd,rthd->rhgt/dot_general | solution.py:67
  65.2 1.3 fusion.13
  66.9 17.9 %psum.7 = bf16[16,1536]{1,0:T(8,128)(2,1)S(1)} all-reduce(bf16[16,1536]{1,0:T(8,128)(2,1)S(1)} %convolution_convert_fusion.3), channel_id=1, replica_groups=mesh['rep'=2,'req'=32,'tp'=4] {'tp'}, use_global_device_ids=true, to_apply=%region_3.4 | all-reduce | flops 24576 | bytes 98304 | tf_op jit(solution)/shard_map/psum | solution.py:92
  84.9 1.5 convolution_convert_fusion
  86.4 2.2 reshape.232
  88.6 51.9 %all_to_all.15 = bf16[64,6,1536]{2,1,0:T(8,128)(2,1)} all-to-all(bf16[64,6,1536]{2,1,0:T(8,128)(2,1)S(1)} %reshape.232), channel_id=1, replica_groups=mesh['rep'=2,'req'=32,'tp'=4] {'rep','req'}, dimensions={0} | all-to-all | bytes 2359296 | tf_op jit(solution)/shard_map/all_to_all | solution.py:164
  140.5 2.3 %reshape.233 = bf16[384,1536]{1,0:T(8,128)(2,1)S(1)} reshape(bf16[64,6,1536]{2,1,0:T(8,128)(2,1)} %all_to_all.15) | data formatting | bytes 2359296 | tf_op jit(solution)/shard_map/reshape | solution.py:166
  142.8 1.7 fusion.16
  145.7 45.9 %all_to_all.16 = bf16[64,6,1536]{2,1,0:T(8,128)(2,1)S(1)} all-to-all(bf16[64,6,1536]{2,1,0:T(8,128)(2,1)S(1)} %copy.76), channel_id=1, replica_groups=mesh['rep'=2,'req'=32,'tp'=4] {'rep','req'}, dimensions={0} | all-to-all | bytes 2359296 | tf_op jit(solution)/shard_map/all_to_all | solution.py:174
  191.7 1.2 reshape.234
  192.9 1.8 convolution_convert_fusion.2
  194.7 0.9 copy.80
  195.7 18.9 %reduce-scatter.4.cloned.1.call-done = bf16[384,16]{1,0:T(8,128)(2,1)} async-done(((bf16[1536,16]{1,0:T(8,128)(2,1)}), bf16[384,16]{1,0:T(8,128)(2,1)}) %reduce-scatter.4.cloned.1.call-update) | async-done | bytes 12304
  214.6 1.0 copy.81
  (71 shorter events, 6.9 us)
Async XLA Ops:
  6.5 60.1 %copy-start = (bf16[384,1536]{1,0:T(8,128)(2,1)S(1)}, bf16[384,1536]{1,0:T(8,128)(2,1)}, u32[]{:S(2)}) copy-start(bf16[384,1536]{1,0:T(8,128)(2,1)} %param.21) | copy-start | bytes 3538948
  14.8 24.4 %collective-permute-start = (bf16[1,262528]{1,0:T(2,128)(2,1)}, bf16[1,262528]{1,0:T(2,128)(2,1)}, u32[]{:S(2)}, u32[]{:S(2)}) collective-permute-start(bf16[1,262528]{1,0:T(2,128)(2,1)} %pad_maximum_fusion), channel_id=1, source_target_pairs={{0,128},{128,0},{1,129},{129,1},{2,130},{130,2},{3,131},{131,3},{4... | collective-permute-start | bytes 1575176 | tf_op jit(solution)/shard_map/ppermute | solution.py:13
  14.8 21.2 %copy-start.5 = (f32[1536]{0:T(1024)S(1)}, f32[1536]{0:T(1024)}, u32[]{:S(2)}) copy-start(f32[1536]{0:T(1024)} %param.17) | copy-start | bytes 18436
  14.8 21.2 %copy-start.2 = (bf16[1536,256]{1,0:T(8,128)(2,1)S(1)}, bf16[1536,256]{1,0:T(8,128)(2,1)}, u32[]{:S(2)}) copy-start(bf16[1536,256]{1,0:T(8,128)(2,1)} %param.20) | copy-start | bytes 2359300
  36.3 1.6 copy-start.6
  36.3 2.3 %copy-start.7 = (f32[16,8]{0,1:T(8,128)S(1)}, f32[16,8]{0,1:T(8,128)}, u32[]{:S(2)}) copy-start(f32[16,8]{0,1:T(8,128)} %param.25) | copy-start | bytes 1540
  36.3 2.6 %copy-start.8 = (s32[2,16]{1,0:T(2,128)S(1)}, s32[2,16]{1,0:T(2,128)}, u32[]{:S(2)}) copy-start(s32[2,16]{1,0:T(2,128)} %param.14) | copy-start | bytes 388
  40.5 18.8 %all-to-all-start = ((bf16[4,16,384]{2,1,0:T(8,128)(2,1)}), bf16[4,16,384]{2,1,0:T(8,128)(2,1)S(1)}, u32[]{:S(2)}, u32[]{:S(2)}) async-start(bf16[4,16,384]{2,1,0:T(8,128)(2,1)} %stack.2), calls=%async_computation | async-start | bytes 98304 | tf_op jit(solution)/shard_map/all_to_all | solution.py:42
  44.8 169.8 %reduce-scatter.4.cloned.1.call-start = ((), (), s32[]{:S(2)}) async-start(), calls=%async_computation.4 | async-start | bytes 491520
  59.6 5.6 %copy-start.1 = (bf16[16,1024,2,128]{1,3,2,0:T(8,128)(2,1)S(1)}, bf16[16,1024,2,128]{1,3,2,0:T(8,128)(2,1)}, u32[]{:S(2)}) copy-start(bf16[16,1024,2,128]{1,3,2,0:T(8,128)(2,1)} %constant_dynamic-update-slice_fusion) | copy-start | bytes 25165828
  66.5 18.4 %copy-start.4 = (f32[1536]{0:T(1024)S(1)}, f32[1536]{0:T(1024)}, u32[]{:S(2)}) copy-start(f32[1536]{0:T(1024)} %param.18) | copy-start | bytes 18436
  142.8 1.8 copy-start.3
Sparse Core Ops, SparseCore 0:
  195.8 18.7 reduce-scatter.3
